TPU v7x, 256 devices: a whole 4x4x8 slice. The times are simulated.
256 devices in a mesh: prop: 8 (over x, core), dom: 32 (over z, y).
Axes of the slice: x: 4, y: 4, z: 8, core: 2. Of those that a mesh axis runs over, the one named last changes fastest.
Arguments:
- states: float32 [8, 128, 64, 128], P('prop', 'dom'), may hold values from -4 to 4
- accepted: int32 [1], replicated, may hold values from 0 to 7
- noise: float32 [8, 128, 64, 128], P('prop', 'dom'), may hold values from -5 to 5
- source: float32 [128, 64, 128], P('dom'), may hold values from -6 to 6
Outputs:
- pressure: float32 [8, 128, 64, 128], P('prop', 'dom')
All inputs are finite; a program needn't handle non-finite values.
Results may differ from a plain program's by a relative error of at most 0.0003.
Values sent between devices are 32-bit elements; how exact they have to be, the bound alone decides.
A program may use at most 128 MiB of HBM per device.

v0:
```python
import math
import jax
import jax.numpy as jnp
from jax import lax
from jax.sharding import PartitionSpec as P

LEVELS = 4
SWEEPS = 2
COARSE_SWEEPS = 64
OMEGA = 0.7
BETA = 0.4
SHRINK = math.sqrt(1.0 - BETA * BETA)
ZSCALE = 16.0


def padded_2(x, sides, width):
    for axis, dim in sides:
        devices, length = (lax.axis_size(axis), x.shape[dim])
        up = [(i, (i + 1) % devices) for i in range(devices - 1)]
        down = [(j, i) for i, j in up]
        last = lax.slice_in_dim(x, length - width, length, axis=dim)
        initial = lax.slice_in_dim(x, 0, width, axis=dim)
        before = lax.ppermute(last, axis, up)
        after = lax.ppermute(initial, axis, down)
        x = jnp.concatenate([before, x, after], axis=dim)
    return x


def from_root(x, axis, root):
    mine = lax.axis_index(axis) == root
    return lax.psum(jnp.where(mine, x, jnp.zeros_like(x)), axis)


def shift_lower(values, axis):
    axis = values.ndim + axis
    count = values.shape[axis]
    kept = lax.slice_in_dim(values, 0, count - 1, axis=axis)
    return jnp.concatenate(
        [jnp.zeros_like(lax.slice_in_dim(values, 0, 1, axis=axis)), kept], axis=axis
    )


def shift_upper(values, axis):
    axis = values.ndim + axis
    count = values.shape[axis]
    kept = lax.slice_in_dim(values, 1, count, axis=axis)
    return jnp.concatenate(
        [kept, jnp.zeros_like(lax.slice_in_dim(values, 0, 1, axis=axis))], axis=axis
    )


def harmonic(first, second):
    return 2.0 * first * second / (first + second)


def coefficients(perm, padded, scale):
    inner_x = harmonic(perm[..., 1:, :], perm[..., :-1, :])
    west = jnp.concatenate([perm[..., :1, :], inner_x], axis=-2)
    east = jnp.concatenate([inner_x, perm[..., -1:, :]], axis=-2)
    inner_y = harmonic(perm[..., 1:], perm[..., :-1])
    south = jnp.concatenate([perm[..., :1], inner_y], axis=-1)
    north = jnp.concatenate([inner_y, perm[..., -1:]], axis=-1)
    below = harmonic(padded[..., :-2, :, :], perm)
    above = harmonic(padded[..., 2:, :, :], perm)
    zfactor = ZSCALE * scale
    parts = [
        west * scale,
        east * scale,
        south * scale,
        north * scale,
        below * zfactor,
        above * zfactor,
    ]
    diagonal = parts[0] + parts[1] + parts[2] + parts[3] + parts[4] + parts[5]
    return parts + [diagonal, OMEGA / diagonal]


def apply_op(values, padded, coefs):
    result = (
        coefs[6] * values - coefs[0] * shift_lower(values, -2) - coefs[1] * shift_upper(values, -2)
    )
    result = result - coefs[2] * shift_lower(values, -1) - coefs[3] * shift_upper(values, -1)
    return result - coefs[4] * padded[..., :-2, :, :] - coefs[5] * padded[..., 2:, :, :]


def sweep(values, right, coefs, pad_z):
    return values + coefs[7] * (right - apply_op(values, pad_z(values), coefs))


def sum_children(values):
    shape = values.shape
    split = values.reshape(shape[:-3] + (shape[-3] // 2, 2, shape[-2] // 2, 2, shape[-1] // 2, 2))
    return split.sum(axis=(-5, -3, -1))


def prolong(values):
    return jnp.repeat(jnp.repeat(jnp.repeat(values, 2, axis=-3), 2, axis=-2), 2, axis=-1)


def zero_pad(values):
    widths = [(0, 0)] * (values.ndim - 3) + [(1, 1), (0, 0), (0, 0)]
    return jnp.pad(values, widths)


def pressure_rim(values):
    return padded_2(values, (("dom", 1),), 1)


def perm_rim(values):
    return padded_2(values, (("dom", 1),), 1)


def coarse_solve(right, perm, level, pad_z, pad_perm):
    coefs = coefficients(perm, pad_perm(perm), 4.0**level)
    start = coefs[7] * right
    return lax.fori_loop(
        0, COARSE_SWEEPS - 1, lambda step, values: sweep(values, right, coefs, pad_z), start
    )


def level_cycle(right, perm, level, pad_z, pad_perm, deeper):
    coefs = coefficients(perm, pad_perm(perm), 4.0**level)
    values = coefs[7] * right
    values = sweep(values, right, coefs, pad_z)
    residue = right - apply_op(values, pad_z(values), coefs)
    update = deeper(sum_children(residue), sum_children(perm) * 0.125, level + 1)
    values = values + prolong(update)
    for step in range(SWEEPS):
        values = sweep(values, right, coefs, pad_z)
    return values


def local_cycle(right, perm, level):
    if level == LEVELS - 1:
        return coarse_solve(right, perm, level, zero_pad, zero_pad)
    return level_cycle(right, perm, level, zero_pad, zero_pad, local_cycle)


def body(states, accepted, noise, source):
    per_device = states.shape[0]
    chosen = accepted[0]
    owner = chosen // per_device
    picked = lax.dynamic_index_in_dim(states, chosen % per_device, 0, keepdims=False)
    current = from_root(picked, "prop", owner)
    theta = SHRINK * current[None] + BETA * noise
    perm = jnp.exp(theta)
    right = source[None]
    gather_level = 2

    def spread_cycle(right_side, field, level):
        if level == gather_level:
            whole_right, whole_perm = (
                lax.all_gather(right_side, "dom", axis=1, tiled=True),
                lax.all_gather(field, "dom", axis=1, tiled=True),
            )
            result = local_cycle(whole_right, whole_perm, level)
            height = right_side.shape[1]
            return lax.dynamic_slice_in_dim(result, lax.axis_index("dom") * height, height, 1)
        return level_cycle(right_side, field, level, pressure_rim, perm_rim, spread_cycle)

    return spread_cycle(right, perm, 0)


def solution(mesh):
    in_specs = (
        P("prop", "dom", None, None),
        P(),
        P("prop", "dom", None, None),
        P("dom", None, None),
    )
    out_specs = P("prop", "dom", None, None)
    return jax.shard_map(body, mesh=mesh, in_specs=in_specs, out_specs=out_specs, check_vma=False)
```

profile of v0, /device:TPU:120, one launch (start us, length us, event | category | flops | bytes accessed | tf_op | source)
XLA Modules:
  0.0 459.8 jit_solution(12875724920466572557)
XLA Ops:
  11.1 65.1 %all-reduce.61.cloned.1.call-done = f32[4,64,128]{1,2,0:T(8,128)} async-done(((f32[4,64,128]{1,2,0:T(8,128)}), f32[4,64,128]{1,2,0:T(8,128)}) %all-reduce.61.cloned.1.call-update) | async-done | bytes 131088 | tf_op jit(solution)/shard_map/psum | solution.py:31
  78.3 9.8 %reshape.767 = f32[2,2,32,2,64,2]{5,4,3,2,1,0:T(8,128)} reshape(f32[1,4,64,128]{3,2,1,0:T(8,128)S(1)} %copy.50) | data formatting | bytes 262144 | tf_op jit(solution)/shard_map/reshape | solution.py:92
  88.1 4.0 reduce_sum.74
  94.8 48.6 %all-gather = f32[512,32]{1,0:T(8,128)S(1)} all-gather(f32[16,32]{1,0:T(8,128)S(1)} %broadcast_multiply_fusion), channel_id=2, replica_groups=mesh['prop'=8,'dom'=32] {'dom'}, dimensions={0}, use_global_device_ids=true | all-gather | bytes 67584 | tf_op jit(solution)/shard_map/all_gather | solution.py:154
  145.8 5.5 %reshape.769 = f32[16,2,8,2,16,2]{3,2,1,0,5,4:T(8,128)} reshape(f32[512,32]{0,1:T(8,128)S(1)} %copy.52) | data formatting | bytes 131072 | tf_op jit(solution)/shard_map/reshape | solution.py:92
  151.4 2.6 reduce_sum.84
  154.2 4.6 collective-permute-start
  158.8 1.9 collective-permute-start.1
  160.8 7.2 %collective-permute-start.4 = (f32[1,1,32,64]{3,2,1,0:T(8,128)}, f32[1,1,32,64]{3,2,1,0:T(8,128)S(1)}, u32[]{:S(2)}, u32[]{:S(2)}) collective-permute-start(f32[1,1,32,64]{3,2,1,0:T(8,128)} %get-tuple-element.298), channel_id=1, source_target_pairs={{0,1},{1,2},{2,3},{3,4},{4,5},{5,6},{6,7},{7,8},{8,9},{9,10},{10,1... | collective-permute-start | bytes 24584 | tf_op jit(solution)/shard_map/ppermute | solution.py:23
  168.0 1.9 collective-permute-start.5
  171.5 1.6 copy.56
  173.2 1.6 copy.57
  179.0 7.2 %collective-permute-start.2 = (f32[1,1,64,128]{2,3,1,0:T(8,128)S(1)}, f32[1,1,64,128]{2,3,1,0:T(8,128)S(1)}, u32[]{:S(2)}, u32[]{:S(2)}) collective-permute-start(f32[1,1,64,128]{2,3,1,0:T(8,128)S(1)} %get-tuple-element.255), channel_id=1, source_target_pairs={{0,1},{1,2},{2,3},{3,4},{4,5},{5,6},{6,7},{7,8},{8,9},{9,10},{10,1... | collective-permute-start | bytes 98312 | tf_op jit(solution)/shard_map/ppermute | solution.py:23
  186.2 1.9 collective-permute-start.3
  188.2 7.5 %collective-permute-done.3 = f32[1,1,64,128]{2,3,1,0:T(8,128)S(1)} collective-permute-done((f32[1,1,64,128]{2,3,1,0:T(8,128)S(1)}, f32[1,1,64,128]{2,3,1,0:T(8,128)S(1)}, u32[]{:S(2)}, u32[]{:S(2)}) %collective-permute-start.3) | collective-permute-done | bytes 32800 | tf_op jit(solution)/shard_map/ppermute | solution.py:24
  196.3 1.9 collective-permute-start.6
  198.2 3.9 collective-permute-start.7
  202.4 5.2 %collective-permute-done.7 = f32[1,1,64,128]{2,3,1,0:T(8,128)S(1)} collective-permute-done((f32[1,1,64,128]{2,3,1,0:T(8,128)S(1)}, f32[1,1,64,128]{2,3,1,0:T(8,128)S(1)}, u32[]{:S(2)}, u32[]{:S(2)}) %collective-permute-start.7) | collective-permute-done | bytes 32800 | tf_op jit(solution)/shard_map/ppermute | solution.py:24
  208.2 9.8 %reshape.768 = f32[2,2,32,2,64,2]{5,4,3,2,1,0:T(8,128)} reshape(f32[1,4,64,128]{3,2,1,0:T(8,128)S(1)} %copy.51) | data formatting | bytes 262144 | tf_op jit(solution)/shard_map/reshape | solution.py:92
  218.0 4.0 reduce_sum.75
  222.3 1.9 collective-permute-start.8
  224.2 3.9 collective-permute-start.9
  228.2 4.9 %collective-permute-done.9 = f32[1,1,32,64]{3,2,1,0:T(8,128)S(1)} collective-permute-done((f32[1,1,32,64]{3,2,1,0:T(8,128)S(1)}, f32[1,1,32,64]{3,2,1,0:T(8,128)S(1)}, u32[]{:S(2)}, u32[]{:S(2)}) %collective-permute-start.9) | collective-permute-done | bytes 8224 | tf_op jit(solution)/shard_map/ppermute | solution.py:24
  233.3 1.9 collective-permute-start.10
  235.2 3.9 collective-permute-start.11
  239.2 4.9 %collective-permute-done.11 = f32[1,1,32,64]{3,2,1,0:T(8,128)S(1)} collective-permute-done((f32[1,1,32,64]{3,2,1,0:T(8,128)S(1)}, f32[1,1,32,64]{3,2,1,0:T(8,128)S(1)}, u32[]{:S(2)}, u32[]{:S(2)}) %collective-permute-start.11) | collective-permute-done | bytes 8224 | tf_op jit(solution)/shard_map/ppermute | solution.py:24
  245.0 46.0 %all-gather.1 = f32[512,32]{1,0:T(8,128)S(1)} all-gather(f32[16,32]{1,0:T(8,128)S(1)} %reduce_sum.82), channel_id=3, replica_groups=mesh['prop'=8,'dom'=32] {'dom'}, dimensions={0}, use_global_device_ids=true | all-gather | bytes 67584 | tf_op jit(solution)/shard_map/all_gather | solution.py:153
  291.0 1.6 fusion.107
  294.0 1.8 fusion.17
  295.8 4.5 reshape.770
  300.3 2.5 reduce_sum.85
  303.6 1.6 bitcast_multiply_fusion.2
  306.3 1.6 copy.62
  307.9 84.0 %while.15 = (s32[]{:T(128)}, f32[1,16,8,16]{3,2,1,0:T(8,128)S(1)}, f32[1,16,8,16]{3,2,1,0:T(8,128)}, f32[1,16,8,16]{3,2,1,0:T(8,128)}, f32[1,16,8,16]{3,2,1,0:T(...) while((s32[]{:T(128)}, f32[1,16,8,16]{3,2,1,0:T(8,128)S(1)}, ...), condition=%wide.region_10.11_spmd, body=%wide.region_9.10_spmd.sunk | while | flops 32770 | bytes 195701 | solution.py:116
  309.4 1.2 fusion.158
  312.0 1.2 fusion.158
  314.7 1.2 fusion.158
  317.4 1.2 fusion.158
  332.0 1.2 fusion.158
  334.7 1.2 fusion.158
  337.4 1.2 fusion.158
  340.0 1.2 fusion.158
  342.7 1.2 fusion.158
  357.4 1.2 fusion.158
  360.1 1.2 fusion.158
  362.7 1.2 fusion.158
  365.4 1.2 fusion.158
  368.1 1.2 fusion.158
  382.7 1.2 fusion.158
  385.4 1.2 fusion.158
  394.4 1.8 copy.65
  397.4 1.3 fusion.24
  400.2 4.6 collective-permute-start.12
  404.8 1.9 collective-permute-start.13
  406.8 7.0 %collective-permute-done.13 = f32[1,1,32,64]{3,2,1,0:T(8,128)S(1)} collective-permute-done((f32[1,1,32,64]{3,2,1,0:T(8,128)S(1)}, f32[1,1,32,64]{3,2,1,0:T(8,128)S(1)}, u32[]{:S(2)}, u32[]{:S(2)}) %collective-permute-start.13) | collective-permute-done | bytes 8224 | tf_op jit(solution)/shard_map/ppermute | solution.py:24
  414.7 1.9 collective-permute-start.14
  416.7 3.9 collective-permute-start.15
  420.7 4.9 %collective-permute-done.15 = f32[1,1,32,64]{3,2,1,0:T(8,128)S(1)} collective-permute-done((f32[1,1,32,64]{3,2,1,0:T(8,128)S(1)}, f32[1,1,32,64]{3,2,1,0:T(8,128)S(1)}, u32[]{:S(2)}, u32[]{:S(2)}) %collective-permute-start.15) | collective-permute-done | bytes 8224 | tf_op jit(solution)/shard_map/ppermute | solution.py:24
  426.9 1.9 collective-permute-start.16
  428.8 3.9 collective-permute-start.17
  433.1 5.2 %collective-permute-done.17 = f32[1,1,64,128]{2,3,1,0:T(8,128)S(1)} collective-permute-done((f32[1,1,64,128]{2,3,1,0:T(8,128)S(1)}, f32[1,1,64,128]{2,3,1,0:T(8,128)S(1)}, u32[]{:S(2)}, u32[]{:S(2)}) %collective-permute-start.17) | collective-permute-done | bytes 32800 | tf_op jit(solution)/shard_map/ppermute | solution.py:24
  439.6 1.9 collective-permute-start.18
  441.5 3.9 collective-permute-start.19
  445.8 5.2 %collective-permute-done.19 = f32[1,1,64,128]{2,3,1,0:T(8,128)S(1)} collective-permute-done((f32[1,1,64,128]{2,3,1,0:T(8,128)S(1)}, f32[1,1,64,128]{2,3,1,0:T(8,128)S(1)}, u32[]{:S(2)}, u32[]{:S(2)}) %collective-permute-start.19) | collective-permute-done | bytes 32800 | tf_op jit(solution)/shard_map/ppermute | solution.py:24
  (397 shorter events, 96.6 us)
Async XLA Ops:
  6.5 69.6 %all-reduce.61.cloned.1.call-start = ((), (), s32[]{:S(2)}) async-start(), calls=%async_computation | async-start | bytes 524288 | tf_op jit(solution)/shard_map/psum | solution.py:31
  77.8 129.9 %copy-start.18 = (f32[1,4,64,1]{2,3,1,0:T(1,128)}, f32[1,4,64,1]{2,3,1,0:T(1,128)S(1)}, u32[]{:S(2)}) copy-start(f32[1,4,64,1]{2,3,1,0:T(1,128)S(1)} %get-tuple-element.261) | copy-start | bytes 3076
  77.8 129.9 %copy-start.19 = (f32[1,4,64,1]{2,3,1,0:T(1,128)}, f32[1,4,64,1]{2,3,1,0:T(1,128)S(1)}, u32[]{:S(2)}) copy-start(f32[1,4,64,1]{2,3,1,0:T(1,128)S(1)} %get-tuple-element.262) | copy-start | bytes 3076
  93.3 150.8 %copy-start.8 = (f32[1,2,31,64]{3,2,1,0:T(8,128)}, f32[1,2,31,64]{3,2,1,0:T(8,128)S(1)}, u32[]{:S(2)}) copy-start(f32[1,2,31,64]{3,2,1,0:T(8,128)S(1)} %add_divide_fusion.7) | copy-start | bytes 47620
  154.2 24.2 %collective-permute-start = (f32[1,1,64,128]{2,3,1,0:T(8,128)}, f32[1,1,64,128]{2,3,1,0:T(8,128)S(1)}, u32[]{:S(2)}, u32[]{:S(2)}) collective-permute-start(f32[1,1,64,128]{2,3,1,0:T(8,128)} %get-tuple-element.260), channel_id=1, source_target_pairs={{0,1},{1,2},{2,3},{3,4},{4,5},{5,6},{6,7},{7,8},{8,9},{9,10},{10,1... | collective-permute-start | bytes 98312 | tf_op jit(solution)/shard_map/ppermute | solution.py:23
  158.8 19.6 %collective-permute-start.1 = (f32[1,1,64,128]{2,3,1,0:T(8,128)}, f32[1,1,64,128]{2,3,1,0:T(8,128)S(1)}, u32[]{:S(2)}, u32[]{:S(2)}) collective-permute-start(f32[1,1,64,128]{2,3,1,0:T(8,128)} %get-tuple-element.259), channel_id=1, source_target_pairs={{1,0},{2,1},{3,2},{4,3},{5,4},{6,5},{7,6},{8,7},{9,8},{10,9},{11,1... | collective-permute-start | bytes 98312 | tf_op jit(solution)/shard_map/ppermute | solution.py:24
  160.8 61.3 %collective-permute-start.4 = (f32[1,1,32,64]{3,2,1,0:T(8,128)}, f32[1,1,32,64]{3,2,1,0:T(8,128)S(1)}, u32[]{:S(2)}, u32[]{:S(2)}) collective-permute-start(f32[1,1,32,64]{3,2,1,0:T(8,128)} %get-tuple-element.298), channel_id=1, source_target_pairs={{0,1},{1,2},{2,3},{3,4},{4,5},{5,6},{6,7},{7,8},{8,9},{9,10},{10,1... | collective-permute-start | bytes 24584 | tf_op jit(solution)/shard_map/ppermute | solution.py:23
  168.0 54.1 %collective-permute-start.5 = (f32[1,1,32,64]{3,2,1,0:T(8,128)}, f32[1,1,32,64]{3,2,1,0:T(8,128)S(1)}, u32[]{:S(2)}, u32[]{:S(2)}) collective-permute-start(f32[1,1,32,64]{3,2,1,0:T(8,128)} %get-tuple-element.297), channel_id=1, source_target_pairs={{1,0},{2,1},{3,2},{4,3},{5,4},{6,5},{7,6},{8,7},{9,8},{10,9},{11,1... | collective-permute-start | bytes 24584 | tf_op jit(solution)/shard_map/ppermute | solution.py:24
  170.8 24.9 %copy-start.7 = (f32[1,16,8,16]{2,1,3,0:T(8,128)}, f32[1,16,8,16]{2,1,3,0:T(8,128)S(1)}, u32[]{:S(2)}) copy-start(f32[1,16,8,16]{2,1,3,0:T(8,128)S(1)} %get-tuple-element.188) | copy-start | bytes 24580
  178.5 39.6 %copy-start.1 = (f32[1,1,64,128]{2,3,1,0:T(8,128)}, f32[1,1,64,128]{2,3,1,0:T(8,128)S(1)}, u32[]{:S(2)}) copy-start(f32[1,1,64,128]{2,3,1,0:T(8,128)S(1)} %collective-permute-done) | copy-start | bytes 98308
  178.5 39.6 %copy-start.3 = (f32[1,1,64,128]{2,3,1,0:T(8,128)}, f32[1,1,64,128]{2,3,1,0:T(8,128)S(1)}, u32[]{:S(2)}) copy-start(f32[1,1,64,128]{2,3,1,0:T(8,128)S(1)} %collective-permute-done.1) | copy-start | bytes 98308
  179.0 9.2 %collective-permute-start.2 = (f32[1,1,64,128]{2,3,1,0:T(8,128)S(1)}, f32[1,1,64,128]{2,3,1,0:T(8,128)S(1)}, u32[]{:S(2)}, u32[]{:S(2)}) collective-permute-start(f32[1,1,64,128]{2,3,1,0:T(8,128)S(1)} %get-tuple-element.255), channel_id=1, source_target_pairs={{0,1},{1,2},{2,3},{3,4},{4,5},{5,6},{6,7},{7,8},{8,9},{9,10},{10,1... | collective-permute-start | bytes 98312 | tf_op jit(solution)/shard_map/ppermute | solution.py:23
  186.2 9.5 %collective-permute-start.3 = (f32[1,1,64,128]{2,3,1,0:T(8,128)S(1)}, f32[1,1,64,128]{2,3,1,0:T(8,128)S(1)}, u32[]{:S(2)}, u32[]{:S(2)}) collective-permute-start(f32[1,1,64,128]{2,3,1,0:T(8,128)S(1)} %get-tuple-element.256), channel_id=1, source_target_pairs={{1,0},{2,1},{3,2},{4,3},{5,4},{6,5},{7,6},{8,7},{9,8},{10,9},{11,1... | collective-permute-start | bytes 98312 | tf_op jit(solution)/shard_map/ppermute | solution.py:24
  196.3 6.2 %collective-permute-start.6 = (f32[1,1,64,128]{2,3,1,0:T(8,128)S(1)}, f32[1,1,64,128]{2,3,1,0:T(8,128)S(1)}, u32[]{:S(2)}, u32[]{:S(2)}) collective-permute-start(f32[1,1,64,128]{2,3,1,0:T(8,128)S(1)} %get-tuple-element.249), channel_id=1, source_target_pairs={{0,1},{1,2},{2,3},{3,4},{4,5},{5,6},{6,7},{7,8},{8,9},{9,10},{10,1... | collective-permute-start | bytes 98312 | tf_op jit(solution)/shard_map/ppermute | solution.py:23
  198.2 9.5 %collective-permute-start.7 = (f32[1,1,64,128]{2,3,1,0:T(8,128)S(1)}, f32[1,1,64,128]{2,3,1,0:T(8,128)S(1)}, u32[]{:S(2)}, u32[]{:S(2)}) collective-permute-start(f32[1,1,64,128]{2,3,1,0:T(8,128)S(1)} %get-tuple-element.250), channel_id=1, source_target_pairs={{1,0},{2,1},{3,2},{4,3},{5,4},{6,5},{7,6},{8,7},{9,8},{10,9},{11,1... | collective-permute-start | bytes 98312 | tf_op jit(solution)/shard_map/ppermute | solution.py:24
  208.2 13.9 %copy-start.17 = (f32[1,2,32,1]{3,2,1,0:T(8,128)S(1)}, f32[1,2,32,1]{3,2,1,0:T(8,128)}, u32[]{:S(2)}) copy-start(f32[1,2,32,1]{3,2,1,0:T(8,128)} %get-tuple-element.296) | copy-start | bytes 772
  208.2 13.9 %copy-start.20 = (f32[1,2,1,64]{3,2,1,0:T(1,128)S(1)}, f32[1,2,1,64]{3,2,1,0:T(1,128)}, u32[]{:S(2)}) copy-start(f32[1,2,1,64]{3,2,1,0:T(1,128)} %get-tuple-element.299) | copy-start | bytes 1540
  208.2 13.9 %copy-start.21 = (f32[1,2,1,64]{3,2,1,0:T(1,128)S(1)}, f32[1,2,1,64]{3,2,1,0:T(1,128)}, u32[]{:S(2)}) copy-start(f32[1,2,1,64]{3,2,1,0:T(1,128)} %get-tuple-element.300) | copy-start | bytes 1540
  222.0 73.8 %copy-start.5 = (f32[2,32,64]{2,1,0:T(8,128)}, f32[2,32,64]{2,1,0:T(8,128)S(1)}, u32[]{:S(2)}) copy-start(f32[2,32,64]{2,1,0:T(8,128)S(1)} %reduce_sum.75) | copy-start | bytes 49156
  222.1 22.1 %copy-start.15 = (f32[1,1,32,64]{3,2,1,0:T(8,128)}, f32[1,1,32,64]{3,2,1,0:T(8,128)S(1)}, u32[]{:S(2)}) copy-start(f32[1,1,32,64]{3,2,1,0:T(8,128)S(1)} %collective-permute-done.4) | copy-start | bytes 24580
  222.1 22.1 %copy-start.16 = (f32[1,1,32,64]{3,2,1,0:T(8,128)}, f32[1,1,32,64]{3,2,1,0:T(8,128)S(1)}, u32[]{:S(2)}) copy-start(f32[1,1,32,64]{3,2,1,0:T(8,128)S(1)} %collective-permute-done.5) | copy-start | bytes 24580
  222.2 21.9 %copy-start.10 = (f32[1,2,32,64]{3,2,1,0:T(8,128)}, f32[1,2,32,64]{3,2,1,0:T(8,128)S(1)}, u32[]{:S(2)}) copy-start(f32[1,2,32,64]{3,2,1,0:T(8,128)S(1)} %get-tuple-element.200) | copy-start | bytes 49156
  222.2 21.9 %copy-start.12 = (f32[1,2,32,64]{3,2,1,0:T(8,128)}, f32[1,2,32,64]{3,2,1,0:T(8,128)S(1)}, u32[]{:S(2)}) copy-start(f32[1,2,32,64]{3,2,1,0:T(8,128)S(1)} %get-tuple-element.201) | copy-start | bytes 49156
  222.3 5.9 %collective-permute-start.8 = (f32[1,1,32,64]{3,2,1,0:T(8,128)S(1)}, f32[1,1,32,64]{3,2,1,0:T(8,128)S(1)}, u32[]{:S(2)}, u32[]{:S(2)}) collective-permute-start(f32[1,1,32,64]{3,2,1,0:T(8,128)S(1)} %get-tuple-element.293), channel_id=1, source_target_pairs={{0,1},{1,2},{2,3},{3,4},{4,5},{5,6},{6,7},{7,8},{8,9},{9,10},{10,1... | collective-permute-start | bytes 24584 | tf_op jit(solution)/shard_map/ppermute | solution.py:23
  224.2 9.0 %collective-permute-start.9 = (f32[1,1,32,64]{3,2,1,0:T(8,128)S(1)}, f32[1,1,32,64]{3,2,1,0:T(8,128)S(1)}, u32[]{:S(2)}, u32[]{:S(2)}) collective-permute-start(f32[1,1,32,64]{3,2,1,0:T(8,128)S(1)} %get-tuple-element.294), channel_id=1, source_target_pairs={{1,0},{2,1},{3,2},{4,3},{5,4},{6,5},{7,6},{8,7},{9,8},{10,9},{11,1... | collective-permute-start | bytes 24584 | tf_op jit(solution)/shard_map/ppermute | solution.py:24
  233.3 5.9 %collective-permute-start.10 = (f32[1,1,32,64]{3,2,1,0:T(8,128)S(1)}, f32[1,1,32,64]{3,2,1,0:T(8,128)S(1)}, u32[]{:S(2)}, u32[]{:S(2)}) collective-permute-start(f32[1,1,32,64]{3,2,1,0:T(8,128)S(1)} %get-tuple-element.287), channel_id=1, source_target_pairs={{0,1},{1,2},{2,3},{3,4},{4,5},{5,6},{6,7},{7,8},{8,9},{9,10},{10,1... | collective-permute-start | bytes 24584 | tf_op jit(solution)/shard_map/ppermute | solution.py:23
  235.2 9.0 %collective-permute-start.11 = (f32[1,1,32,64]{3,2,1,0:T(8,128)S(1)}, f32[1,1,32,64]{3,2,1,0:T(8,128)S(1)}, u32[]{:S(2)}, u32[]{:S(2)}) collective-permute-start(f32[1,1,32,64]{3,2,1,0:T(8,128)S(1)} %get-tuple-element.288), channel_id=1, source_target_pairs={{1,0},{2,1},{3,2},{4,3},{5,4},{6,5},{7,6},{8,7},{9,8},{10,9},{11,1... | collective-permute-start | bytes 24584 | tf_op jit(solution)/shard_map/ppermute | solution.py:24
  292.6 1.3 copy-start
  396.2 2.8 copy-start.14
  397.2 16.7 %copy-start.6 = (f32[2,32,64]{2,1,0:T(8,128)S(1)}, f32[2,32,64]{2,1,0:T(8,128)}, u32[]{:S(2)}) copy-start(f32[2,32,64]{2,1,0:T(8,128)} %copy-done.5) | copy-start | bytes 49156
  397.2 16.6 %copy-start.9 = (f32[1,2,31,64]{3,2,1,0:T(8,128)S(1)}, f32[1,2,31,64]{3,2,1,0:T(8,128)}, u32[]{:S(2)}) copy-start(f32[1,2,31,64]{3,2,1,0:T(8,128)} %copy-done.8) | copy-start | bytes 47620
  397.2 16.6 %copy-start.11 = (f32[1,2,32,64]{3,2,1,0:T(8,128)S(1)}, f32[1,2,32,64]{3,2,1,0:T(8,128)}, u32[]{:S(2)}) copy-start(f32[1,2,32,64]{3,2,1,0:T(8,128)} %copy-done.10) | copy-start | bytes 49156
  397.2 16.6 %copy-start.13 = (f32[1,2,32,64]{3,2,1,0:T(8,128)S(1)}, f32[1,2,32,64]{3,2,1,0:T(8,128)}, u32[]{:S(2)}) copy-start(f32[1,2,32,64]{3,2,1,0:T(8,128)} %copy-done.12) | copy-start | bytes 49156
  397.3 41.0 %copy-start.2 = (f32[1,1,64,128]{2,3,1,0:T(8,128)S(1)}, f32[1,1,64,128]{2,3,1,0:T(8,128)}, u32[]{:S(2)}) copy-start(f32[1,1,64,128]{2,3,1,0:T(8,128)} %copy-done.1) | copy-start | bytes 98308
  397.3 41.0 %copy-start.4 = (f32[1,1,64,128]{2,3,1,0:T(8,128)S(1)}, f32[1,1,64,128]{2,3,1,0:T(8,128)}, u32[]{:S(2)}) copy-start(f32[1,1,64,128]{2,3,1,0:T(8,128)} %copy-done.3) | copy-start | bytes 98308
  400.2 6.6 %collective-permute-start.12 = (f32[1,1,32,64]{3,2,1,0:T(8,128)S(1)}, f32[1,1,32,64]{3,2,1,0:T(8,128)S(1)}, u32[]{:S(2)}, u32[]{:S(2)}) collective-permute-start(f32[1,1,32,64]{3,2,1,0:T(8,128)S(1)} %get-tuple-element.279), channel_id=1, source_target_pairs={{0,1},{1,2},{2,3},{3,4},{4,5},{5,6},{6,7},{7,8},{8,9},{9,10},{10,1... | collective-permute-start | bytes 24584 | tf_op jit(solution)/shard_map/ppermute | solution.py:23
  404.8 9.0 %collective-permute-start.13 = (f32[1,1,32,64]{3,2,1,0:T(8,128)S(1)}, f32[1,1,32,64]{3,2,1,0:T(8,128)S(1)}, u32[]{:S(2)}, u32[]{:S(2)}) collective-permute-start(f32[1,1,32,64]{3,2,1,0:T(8,128)S(1)} %get-tuple-element.280), channel_id=1, source_target_pairs={{1,0},{2,1},{3,2},{4,3},{5,4},{6,5},{7,6},{8,7},{9,8},{10,9},{11,1... | collective-permute-start | bytes 24584 | tf_op jit(solution)/shard_map/ppermute | solution.py:24
  414.7 5.9 %collective-permute-start.14 = (f32[1,1,32,64]{3,2,1,0:T(8,128)S(1)}, f32[1,1,32,64]{3,2,1,0:T(8,128)S(1)}, u32[]{:S(2)}, u32[]{:S(2)}) collective-permute-start(f32[1,1,32,64]{3,2,1,0:T(8,128)S(1)} %get-tuple-element.273), channel_id=1, source_target_pairs={{0,1},{1,2},{2,3},{3,4},{4,5},{5,6},{6,7},{7,8},{8,9},{9,10},{10,1... | collective-permute-start | bytes 24584 | tf_op jit(solution)/shard_map/ppermute | solution.py:23
  416.7 9.0 %collective-permute-start.15 = (f32[1,1,32,64]{3,2,1,0:T(8,128)S(1)}, f32[1,1,32,64]{3,2,1,0:T(8,128)S(1)}, u32[]{:S(2)}, u32[]{:S(2)}) collective-permute-start(f32[1,1,32,64]{3,2,1,0:T(8,128)S(1)} %get-tuple-element.274), channel_id=1, source_target_pairs={{1,0},{2,1},{3,2},{4,3},{5,4},{6,5},{7,6},{8,7},{9,8},{10,9},{11,1... | collective-permute-start | bytes 24584 | tf_op jit(solution)/shard_map/ppermute | solution.py:24
  426.9 6.2 %collective-permute-start.16 = (f32[1,1,64,128]{2,3,1,0:T(8,128)S(1)}, f32[1,1,64,128]{2,3,1,0:T(8,128)S(1)}, u32[]{:S(2)}, u32[]{:S(2)}) collective-permute-start(f32[1,1,64,128]{2,3,1,0:T(8,128)S(1)} %get-tuple-element.219), channel_id=1, source_target_pairs={{0,1},{1,2},{2,3},{3,4},{4,5},{5,6},{6,7},{7,8},{8,9},{9,10},{10,1... | collective-permute-start | bytes 98312 | tf_op jit(solution)/shard_map/ppermute | solution.py:23
  428.8 9.5 %collective-permute-start.17 = (f32[1,1,64,128]{2,3,1,0:T(8,128)S(1)}, f32[1,1,64,128]{2,3,1,0:T(8,128)S(1)}, u32[]{:S(2)}, u32[]{:S(2)}) collective-permute-start(f32[1,1,64,128]{2,3,1,0:T(8,128)S(1)} %get-tuple-element.220), channel_id=1, source_target_pairs={{1,0},{2,1},{3,2},{4,3},{5,4},{6,5},{7,6},{8,7},{9,8},{10,9},{11,1... | collective-permute-start | bytes 98312 | tf_op jit(solution)/shard_map/ppermute | solution.py:24
  439.6 6.2 %collective-permute-start.18 = (f32[1,1,64,128]{2,3,1,0:T(8,128)S(1)}, f32[1,1,64,128]{2,3,1,0:T(8,128)S(1)}, u32[]{:S(2)}, u32[]{:S(2)}) collective-permute-start(f32[1,1,64,128]{2,3,1,0:T(8,128)S(1)} %get-tuple-element.213), channel_id=1, source_target_pairs={{0,1},{1,2},{2,3},{3,4},{4,5},{5,6},{6,7},{7,8},{8,9},{9,10},{10,1... | collective-permute-start | bytes 98312 | tf_op jit(solution)/shard_map/ppermute | solution.py:23
  441.5 9.5 %collective-permute-start.19 = (f32[1,1,64,128]{2,3,1,0:T(8,128)S(1)}, f32[1,1,64,128]{2,3,1,0:T(8,128)S(1)}, u32[]{:S(2)}, u32[]{:S(2)}) collective-permute-start(f32[1,1,64,128]{2,3,1,0:T(8,128)S(1)} %get-tuple-element.214), channel_id=1, source_target_pairs={{1,0},{2,1},{3,2},{4,3},{5,4},{6,5},{7,6},{8,7},{9,8},{10,9},{11,1... | collective-permute-start | bytes 98312 | tf_op jit(solution)/shard_map/ppermute | solution.py:24
Sparse Core Ops, SparseCore 0:
  9.7 66.4 all-reduce.60
where the time goes:
time: 465 us; the launch traced here: 460 us
  waiting for transfers between devices  111 us (24%)
  other arithmetic  108 us (23%)
  blocking collectives  94.6 us (20%)
  starting transfers between devices  66.4 us (14%)
  local copies, waits for them, and re-layouts  62.8 us (14%)
  between operations  15 us (3%)
    add x71, other arithmetic, sweep(): return values + coefs[7] * (right - apply_op(values, pad_z(values), coefs))  82.6 us
    psum x1, waiting for transfers between devices, from_root(): return lax.psum(jnp.where(mine, x, jnp.zeros_like(x)), axis)  65.1 us
    all_gather x1, blocking collectives, spread_cycle(): lax.all_gather(field, 'dom', axis=1, tiled=True)  48.6 us
    all_gather x1, blocking collectives, spread_cycle(): lax.all_gather(right_side, 'dom', axis=1, tiled=True)  46 us
    ppermute x10, waiting for transfers between devices, padded_2(): after = lax.ppermute(initial, axis, down)  45.1 us
    ppermute x10, starting transfers between devices, padded_2(): before = lax.ppermute(last, axis, up)  35.2 us
    ppermute x10, starting transfers between devices, padded_2(): after = lax.ppermute(initial, axis, down)  31.2 us
    reshape x4, local copies, waits for them, and re-layouts, sum_children(): values.reshape(shape[:-3] + (shape[-3] // 2, 2, shape[-2] // 2, 2, shape[...  29.6 us
  transfers between devices with their start and end apart: 21, of which 12 were waited for; matrix products, arithmetic and copies ran while one was open for 6% of the time, Pallas kernels for 0%

commit v1 on v0

--- a/solution.py
+++ b/solution.py
@@ -151,7 +151,9 @@
         if level == gather_level:
             whole_right, whole_perm = (
                 lax.all_gather(right_side, "dom", axis=1, tiled=True),
-                lax.all_gather(field, "dom", axis=1, tiled=True),
+                jnp.concatenate(
+                    lax.all_to_all(jnp.stack([field] * lax.axis_size("dom")), "dom", 0, 0), axis=1
+                ),
             )
             result = local_cycle(whole_right, whole_perm, level)
             height = right_side.shape[1]

time: 465 us -> 412 us (0.89)
  blocking collectives: 94.6 us -> 46 us
  local copies, waits for them, and re-layouts: 62.8 us -> 49.6 us
  starting transfers between devices: 66.4 us -> 73.8 us
    all_gather x1 -> x0, blocking collectives: 48.6 us -> none  [spread_cycle(): lax.all_gather(field, 'dom', axis=1, tiled=True)]
    while x73 -> x63, local copies, waits for them, and re-layouts: 10.7 us -> 0.4 us  [the longest x10 10.3 us: coarse_solve(): lax.fori_loop(0, COARSE_SWEEPS - 1, lambda step, values: sweep(values, ri...]
    all_to_all x0 -> x1, starting transfers between devices: none -> 10.1 us  [spread_cycle(): lax.all_to_all(jnp.stack([field] * lax.axis_size('dom')), 'dom', 0, 0)]
    reshape x4 -> x3, local copies, waits for them, and re-layouts: 29.6 us -> 23.2 us  [sum_children(): values.reshape(shape[:-3] + (shape[-3] // 2, 2, shape[-2] // 2, 2, shape[...]
  transfers between devices with their start and end apart: 21 -> 22, of which waited for: 12 -> 12; matrix products, arithmetic and copies ran while one was open for 6% -> 5% of each run, Pallas kernels for 0% -> 0%
where the time goes in v1:
time: 412 us; the launch traced here: 407 us
  waiting for transfers between devices  111 us (27%)
  other arithmetic  109 us (26%)
  starting transfers between devices  73.8 us (18%)
  local copies, waits for them, and re-layouts  49.6 us (12%)
  blocking collectives  46 us (11%)
  between operations  15 us (4%)
    add x71, other arithmetic, sweep(): return values + coefs[7] * (right - apply_op(values, pad_z(values), coefs))  81.9 us
    psum x1, waiting for transfers between devices, from_root(): return lax.psum(jnp.where(mine, x, jnp.zeros_like(x)), axis)  65.1 us
    all_gather x1, blocking collectives, spread_cycle(): lax.all_gather(right_side, 'dom', axis=1, tiled=True)  46 us
    ppermute x10, waiting for transfers between devices, padded_2(): after = lax.ppermute(initial, axis, down)  45.3 us
    ppermute x10, starting transfers between devices, padded_2(): before = lax.ppermute(last, axis, up)  32.5 us
    ppermute x10, starting transfers between devices, padded_2(): after = lax.ppermute(initial, axis, down)  31.2 us
    reshape x3, local copies, waits for them, and re-layouts, sum_children(): values.reshape(shape[:-3] + (shape[-3] // 2, 2, shape[-2] // 2, 2, shape[...  23.2 us
    reduce_sum x8, other arithmetic, sum_children(): return split.sum(axis=(-5, -3, -1))  14.2 us
  transfers between devices with their start and end apart: 22, of which 12 were waited for; matrix products, arithmetic and copies ran while one was open for 5% of the time, Pallas kernels for 0%

profile of v1, /device:TPU:120, one launch (start us, length us, event | category | flops | bytes accessed | tf_op | source)
XLA Modules:
  0.0 406.6 jit_solution(666236880155346609)
XLA Ops:
  11.1 65.1 %all-reduce.61.cloned.1.call-done = f32[4,64,128]{1,2,0:T(8,128)} async-done(((f32[4,64,128]{1,2,0:T(8,128)}), f32[4,64,128]{1,2,0:T(8,128)}) %all-reduce.61.cloned.1.call-update) | async-done | bytes 131088 | tf_op jit(solution)/shard_map/psum | solution.py:31
  77.7 9.8 %reshape.764 = f32[2,2,32,2,64,2]{5,4,3,2,1,0:T(8,128)} reshape(f32[1,4,64,128]{3,2,1,0:T(8,128)S(1)} %copy.28) | data formatting | bytes 262144 | tf_op jit(solution)/shard_map/reshape | solution.py:92
  87.5 4.0 reduce_sum.74
  91.8 4.6 %collective-permute-start = (f32[1,1,64,128]{2,3,1,0:T(8,128)S(1)}, f32[1,1,64,128]{2,3,1,0:T(8,128)S(1)}, u32[]{:S(2)}, u32[]{:S(2)}) collective-permute-start(f32[1,1,64,128]{2,3,1,0:T(8,128)S(1)} %get-tuple-element.240), channel_id=1, source_target_pairs={{0,1},{1,2},{2,3},{3,4},{4,5},{5,6},{6,7},{7,8},{8,9},{9,10},{10,1... | collective-permute-start | bytes 98312 | tf_op jit(solution)/shard_map/ppermute | solution.py:23
  96.4 1.9 collective-permute-start.1
  98.3 7.2 %collective-permute-start.4 = (f32[1,1,32,64]{3,2,1,0:T(8,128)S(1)}, f32[1,1,32,64]{3,2,1,0:T(8,128)S(1)}, u32[]{:S(2)}, u32[]{:S(2)}) collective-permute-start(f32[1,1,32,64]{3,2,1,0:T(8,128)S(1)} %get-tuple-element.276), channel_id=1, source_target_pairs={{0,1},{1,2},{2,3},{3,4},{4,5},{5,6},{6,7},{7,8},{8,9},{9,10},{10,1... | collective-permute-start | bytes 24584 | tf_op jit(solution)/shard_map/ppermute | solution.py:23
  105.6 1.9 collective-permute-start.5
  109.0 10.1 %all-to-all-start = ((f32[32,1,512]{2,1,0:T(1,128)}), f32[32,1,512]{2,1,0:T(1,128)}, u32[]{:S(2)}, u32[]{:S(2)}) async-start(f32[32,1,512]{2,1,0:T(1,128)} %reshape.769), calls=%async_computation | async-start | bytes 131072 | tf_op jit(solution)/shard_map/all_to_all | solution.py:155
  119.6 4.6 %collective-permute-start.2 = (f32[1,1,64,128]{2,3,1,0:T(8,128)S(1)}, f32[1,1,64,128]{2,3,1,0:T(8,128)S(1)}, u32[]{:S(2)}, u32[]{:S(2)}) collective-permute-start(f32[1,1,64,128]{2,3,1,0:T(8,128)S(1)} %get-tuple-element.235), channel_id=1, source_target_pairs={{0,1},{1,2},{2,3},{3,4},{4,5},{5,6},{6,7},{7,8},{8,9},{9,10},{10,1... | collective-permute-start | bytes 98312 | tf_op jit(solution)/shard_map/ppermute | solution.py:23
  124.2 1.9 collective-permute-start.3
  126.2 7.5 %collective-permute-done.3 = f32[1,1,64,128]{2,3,1,0:T(8,128)S(1)} collective-permute-done((f32[1,1,64,128]{2,3,1,0:T(8,128)S(1)}, f32[1,1,64,128]{2,3,1,0:T(8,128)S(1)}, u32[]{:S(2)}, u32[]{:S(2)}) %collective-permute-start.3) | collective-permute-done | bytes 32800 | tf_op jit(solution)/shard_map/ppermute | solution.py:24
  134.3 1.9 collective-permute-start.6
  136.2 3.9 collective-permute-start.7
  140.4 5.2 %collective-permute-done.7 = f32[1,1,64,128]{2,3,1,0:T(8,128)S(1)} collective-permute-done((f32[1,1,64,128]{2,3,1,0:T(8,128)S(1)}, f32[1,1,64,128]{2,3,1,0:T(8,128)S(1)}, u32[]{:S(2)}, u32[]{:S(2)}) %collective-permute-start.7) | collective-permute-done | bytes 32800 | tf_op jit(solution)/shard_map/ppermute | solution.py:24
  146.2 9.8 %reshape.765 = f32[2,2,32,2,64,2]{5,4,3,2,1,0:T(8,128)} reshape(f32[1,4,64,128]{3,2,1,0:T(8,128)S(1)} %copy.29) | data formatting | bytes 262144 | tf_op jit(solution)/shard_map/reshape | solution.py:92
  156.0 4.0 reduce_sum.75
  160.2 1.9 collective-permute-start.8
  162.1 3.9 collective-permute-start.9
  166.2 4.9 %collective-permute-done.9 = f32[1,1,32,64]{3,2,1,0:T(8,128)S(1)} collective-permute-done((f32[1,1,32,64]{3,2,1,0:T(8,128)S(1)}, f32[1,1,32,64]{3,2,1,0:T(8,128)S(1)}, u32[]{:S(2)}, u32[]{:S(2)}) %collective-permute-start.9) | collective-permute-done | bytes 8224 | tf_op jit(solution)/shard_map/ppermute | solution.py:24
  171.2 1.9 collective-permute-start.10
  173.1 3.9 collective-permute-start.11
  177.2 4.9 %collective-permute-done.11 = f32[1,1,32,64]{3,2,1,0:T(8,128)S(1)} collective-permute-done((f32[1,1,32,64]{3,2,1,0:T(8,128)S(1)}, f32[1,1,32,64]{3,2,1,0:T(8,128)S(1)}, u32[]{:S(2)}, u32[]{:S(2)}) %collective-permute-start.11) | collective-permute-done | bytes 8224 | tf_op jit(solution)/shard_map/ppermute | solution.py:24
  182.9 46.0 %all-gather = f32[512,32]{1,0:T(8,128)S(1)} all-gather(f32[16,32]{1,0:T(8,128)S(1)} %reduce_sum.82), channel_id=2, replica_groups=mesh['prop'=8,'dom'=32] {'dom'}, dimensions={0}, use_global_device_ids=true | all-gather | bytes 67584 | tf_op jit(solution)/shard_map/all_gather | solution.py:153
  229.4 1.6 reduce.12
  234.5 3.6 reshape_reshape.3
  238.1 2.5 reduce_sum.84
  243.3 1.6 fusion.17
  245.0 3.6 reshape.767
  248.6 3.2 reduce_sum.85
  251.8 1.9 broadcast_divide_fusion
  254.6 84.1 %while.15 = (s32[]{:T(128)}, f32[1,16,8,16]{3,2,1,0:T(8,128)S(1)}, f32[1,16,8,16]{3,2,1,0:T(8,128)}, f32[1,16,8,16]{3,2,1,0:T(8,128)}, f32[1,16,8,16]{3,2,1,0:T(...) while((s32[]{:T(128)}, f32[1,16,8,16]{3,2,1,0:T(8,128)S(1)}, ...), condition=%wide.region_10.11_spmd, body=%wide.region_9.10_spmd.sunk | while | flops 32770 | bytes 195701 | solution.py:116
  254.7 1.2 fusion.159
  256.0 1.2 fusion.159
  257.4 1.2 fusion.159
  260.0 1.2 fusion.159
  274.7 1.2 fusion.159
  277.4 1.2 fusion.159
  280.1 1.2 fusion.159
  282.7 1.2 fusion.159
  285.4 1.2 fusion.159
  300.1 1.2 fusion.159
  302.7 1.2 fusion.159
  305.4 1.2 fusion.159
  308.1 1.2 fusion.159
  310.7 1.2 fusion.159
  325.4 1.2 fusion.159
  328.1 1.2 fusion.159
  330.8 1.2 fusion.159
  333.4 1.2 fusion.159
  336.1 1.2 fusion.159
  341.1 1.8 copy.31
  344.2 1.3 fusion.24
  346.9 4.6 %collective-permute-start.12 = (f32[1,1,32,64]{3,2,1,0:T(8,128)S(1)}, f32[1,1,32,64]{3,2,1,0:T(8,128)S(1)}, u32[]{:S(2)}, u32[]{:S(2)}) collective-permute-start(f32[1,1,32,64]{3,2,1,0:T(8,128)S(1)} %get-tuple-element.257), channel_id=1, source_target_pairs={{0,1},{1,2},{2,3},{3,4},{4,5},{5,6},{6,7},{7,8},{8,9},{9,10},{10,1... | collective-permute-start | bytes 24584 | tf_op jit(solution)/shard_map/ppermute | solution.py:23
  351.5 1.9 collective-permute-start.13
  353.5 7.1 %collective-permute-done.13 = f32[1,1,32,64]{3,2,1,0:T(8,128)S(1)} collective-permute-done((f32[1,1,32,64]{3,2,1,0:T(8,128)S(1)}, f32[1,1,32,64]{3,2,1,0:T(8,128)S(1)}, u32[]{:S(2)}, u32[]{:S(2)}) %collective-permute-start.13) | collective-permute-done | bytes 8224 | tf_op jit(solution)/shard_map/ppermute | solution.py:24
  361.5 1.9 collective-permute-start.14
  363.5 3.9 collective-permute-start.15
  367.5 5.0 %collective-permute-done.15 = f32[1,1,32,64]{3,2,1,0:T(8,128)S(1)} collective-permute-done((f32[1,1,32,64]{3,2,1,0:T(8,128)S(1)}, f32[1,1,32,64]{3,2,1,0:T(8,128)S(1)}, u32[]{:S(2)}, u32[]{:S(2)}) %collective-permute-start.15) | collective-permute-done | bytes 8224 | tf_op jit(solution)/shard_map/ppermute | solution.py:24
  373.8 1.9 collective-permute-start.16
  375.7 3.9 collective-permute-start.17
  380.0 5.2 %collective-permute-done.17 = f32[1,1,64,128]{2,3,1,0:T(8,128)S(1)} collective-permute-done((f32[1,1,64,128]{2,3,1,0:T(8,128)S(1)}, f32[1,1,64,128]{2,3,1,0:T(8,128)S(1)}, u32[]{:S(2)}, u32[]{:S(2)}) %collective-permute-start.17) | collective-permute-done | bytes 32800 | tf_op jit(solution)/shard_map/ppermute | solution.py:24
  386.5 1.9 collective-permute-start.18
  388.4 3.9 collective-permute-start.19
  392.6 5.2 %collective-permute-done.19 = f32[1,1,64,128]{2,3,1,0:T(8,128)S(1)} collective-permute-done((f32[1,1,64,128]{2,3,1,0:T(8,128)S(1)}, f32[1,1,64,128]{2,3,1,0:T(8,128)S(1)}, u32[]{:S(2)}, u32[]{:S(2)}) %collective-permute-start.19) | collective-permute-done | bytes 32800 | tf_op jit(solution)/shard_map/ppermute | solution.py:24
  (395 shorter events, 87.6 us)
Async XLA Ops:
  6.5 69.6 %all-reduce.61.cloned.1.call-start = ((), (), s32[]{:S(2)}) async-start(), calls=%async_computation.1 | async-start | bytes 524288 | tf_op jit(solution)/shard_map/psum | solution.py:31
  77.2 68.5 %copy-start.20 = (f32[1,4,64,1]{2,3,1,0:T(1,128)}, f32[1,4,64,1]{2,3,1,0:T(1,128)S(1)}, u32[]{:S(2)}) copy-start(f32[1,4,64,1]{2,3,1,0:T(1,128)S(1)} %get-tuple-element.241) | copy-start | bytes 3076
  77.2 68.5 %copy-start.21 = (f32[1,4,64,1]{2,3,1,0:T(1,128)}, f32[1,4,64,1]{2,3,1,0:T(1,128)S(1)}, u32[]{:S(2)}) copy-start(f32[1,4,64,1]{2,3,1,0:T(1,128)S(1)} %get-tuple-element.242) | copy-start | bytes 3076
  91.5 90.6 %copy-start.22 = (f32[1,2,1,64]{3,2,1,0:T(1,128)}, f32[1,2,1,64]{3,2,1,0:T(1,128)S(1)}, u32[]{:S(2)}) copy-start(f32[1,2,1,64]{3,2,1,0:T(1,128)S(1)} %get-tuple-element.277) | copy-start | bytes 1540
  91.5 90.6 %copy-start.23 = (f32[1,2,1,64]{3,2,1,0:T(1,128)}, f32[1,2,1,64]{3,2,1,0:T(1,128)S(1)}, u32[]{:S(2)}) copy-start(f32[1,2,1,64]{3,2,1,0:T(1,128)S(1)} %get-tuple-element.278) | copy-start | bytes 1540
  91.6 90.5 %copy-start.10 = (f32[1,2,31,64]{3,2,1,0:T(8,128)}, f32[1,2,31,64]{3,2,1,0:T(8,128)S(1)}, u32[]{:S(2)}) copy-start(f32[1,2,31,64]{3,2,1,0:T(8,128)S(1)} %add_divide_fusion.7) | copy-start | bytes 47620
  91.8 27.3 %collective-permute-start = (f32[1,1,64,128]{2,3,1,0:T(8,128)S(1)}, f32[1,1,64,128]{2,3,1,0:T(8,128)S(1)}, u32[]{:S(2)}, u32[]{:S(2)}) collective-permute-start(f32[1,1,64,128]{2,3,1,0:T(8,128)S(1)} %get-tuple-element.240), channel_id=1, source_target_pairs={{0,1},{1,2},{2,3},{3,4},{4,5},{5,6},{6,7},{7,8},{8,9},{9,10},{10,1... | collective-permute-start | bytes 98312 | tf_op jit(solution)/shard_map/ppermute | solution.py:23
  96.4 22.7 %collective-permute-start.1 = (f32[1,1,64,128]{2,3,1,0:T(8,128)S(1)}, f32[1,1,64,128]{2,3,1,0:T(8,128)S(1)}, u32[]{:S(2)}, u32[]{:S(2)}) collective-permute-start(f32[1,1,64,128]{2,3,1,0:T(8,128)S(1)} %get-tuple-element.239), channel_id=1, source_target_pairs={{1,0},{2,1},{3,2},{4,3},{5,4},{6,5},{7,6},{8,7},{9,8},{10,9},{11,1... | collective-permute-start | bytes 98312 | tf_op jit(solution)/shard_map/ppermute | solution.py:24
  98.3 61.7 %collective-permute-start.4 = (f32[1,1,32,64]{3,2,1,0:T(8,128)S(1)}, f32[1,1,32,64]{3,2,1,0:T(8,128)S(1)}, u32[]{:S(2)}, u32[]{:S(2)}) collective-permute-start(f32[1,1,32,64]{3,2,1,0:T(8,128)S(1)} %get-tuple-element.276), channel_id=1, source_target_pairs={{0,1},{1,2},{2,3},{3,4},{4,5},{5,6},{6,7},{7,8},{8,9},{9,10},{10,1... | collective-permute-start | bytes 24584 | tf_op jit(solution)/shard_map/ppermute | solution.py:23
  105.6 54.5 %collective-permute-start.5 = (f32[1,1,32,64]{3,2,1,0:T(8,128)S(1)}, f32[1,1,32,64]{3,2,1,0:T(8,128)S(1)}, u32[]{:S(2)}, u32[]{:S(2)}) collective-permute-start(f32[1,1,32,64]{3,2,1,0:T(8,128)S(1)} %get-tuple-element.275), channel_id=1, source_target_pairs={{1,0},{2,1},{3,2},{4,3},{5,4},{6,5},{7,6},{8,7},{9,8},{10,9},{11,1... | collective-permute-start | bytes 24584 | tf_op jit(solution)/shard_map/ppermute | solution.py:24
  109.0 119.9 %all-to-all-start = ((f32[32,1,512]{2,1,0:T(1,128)}), f32[32,1,512]{2,1,0:T(1,128)}, u32[]{:S(2)}, u32[]{:S(2)}) async-start(f32[32,1,512]{2,1,0:T(1,128)} %reshape.769), calls=%async_computation | async-start | bytes 131072 | tf_op jit(solution)/shard_map/all_to_all | solution.py:155
  119.1 36.9 %copy-start.4 = (f32[1,1,64,128]{2,3,1,0:T(8,128)}, f32[1,1,64,128]{2,3,1,0:T(8,128)S(1)}, u32[]{:S(2)}) copy-start(f32[1,1,64,128]{2,3,1,0:T(8,128)S(1)} %collective-permute-done) | copy-start | bytes 98308
  119.1 36.9 %copy-start.6 = (f32[1,1,64,128]{2,3,1,0:T(8,128)}, f32[1,1,64,128]{2,3,1,0:T(8,128)S(1)}, u32[]{:S(2)}) copy-start(f32[1,1,64,128]{2,3,1,0:T(8,128)S(1)} %collective-permute-done.1) | copy-start | bytes 98308
  119.6 6.6 %collective-permute-start.2 = (f32[1,1,64,128]{2,3,1,0:T(8,128)S(1)}, f32[1,1,64,128]{2,3,1,0:T(8,128)S(1)}, u32[]{:S(2)}, u32[]{:S(2)}) collective-permute-start(f32[1,1,64,128]{2,3,1,0:T(8,128)S(1)} %get-tuple-element.235), channel_id=1, source_target_pairs={{0,1},{1,2},{2,3},{3,4},{4,5},{5,6},{6,7},{7,8},{8,9},{9,10},{10,1... | collective-permute-start | bytes 98312 | tf_op jit(solution)/shard_map/ppermute | solution.py:23
  124.2 9.5 %collective-permute-start.3 = (f32[1,1,64,128]{2,3,1,0:T(8,128)S(1)}, f32[1,1,64,128]{2,3,1,0:T(8,128)S(1)}, u32[]{:S(2)}, u32[]{:S(2)}) collective-permute-start(f32[1,1,64,128]{2,3,1,0:T(8,128)S(1)} %get-tuple-element.236), channel_id=1, source_target_pairs={{1,0},{2,1},{3,2},{4,3},{5,4},{6,5},{7,6},{8,7},{9,8},{10,9},{11,1... | collective-permute-start | bytes 98312 | tf_op jit(solution)/shard_map/ppermute | solution.py:24
  134.3 6.2 %collective-permute-start.6 = (f32[1,1,64,128]{2,3,1,0:T(8,128)S(1)}, f32[1,1,64,128]{2,3,1,0:T(8,128)S(1)}, u32[]{:S(2)}, u32[]{:S(2)}) collective-permute-start(f32[1,1,64,128]{2,3,1,0:T(8,128)S(1)} %get-tuple-element.229), channel_id=1, source_target_pairs={{0,1},{1,2},{2,3},{3,4},{4,5},{5,6},{6,7},{7,8},{8,9},{9,10},{10,1... | collective-permute-start | bytes 98312 | tf_op jit(solution)/shard_map/ppermute | solution.py:23
  136.2 9.5 %collective-permute-start.7 = (f32[1,1,64,128]{2,3,1,0:T(8,128)S(1)}, f32[1,1,64,128]{2,3,1,0:T(8,128)S(1)}, u32[]{:S(2)}, u32[]{:S(2)}) collective-permute-start(f32[1,1,64,128]{2,3,1,0:T(8,128)S(1)} %get-tuple-element.230), channel_id=1, source_target_pairs={{1,0},{2,1},{3,2},{4,3},{5,4},{6,5},{7,6},{8,7},{9,8},{10,9},{11,1... | collective-permute-start | bytes 98312 | tf_op jit(solution)/shard_map/ppermute | solution.py:24
  160.0 74.5 %copy-start.8 = (f32[2,32,64]{2,1,0:T(8,128)}, f32[2,32,64]{2,1,0:T(8,128)S(1)}, u32[]{:S(2)}) copy-start(f32[2,32,64]{2,1,0:T(8,128)S(1)} %reduce_sum.75) | copy-start | bytes 49156
  160.0 71.3 %copy-start.18 = (f32[1,1,32,64]{3,2,1,0:T(8,128)}, f32[1,1,32,64]{3,2,1,0:T(8,128)S(1)}, u32[]{:S(2)}) copy-start(f32[1,1,32,64]{3,2,1,0:T(8,128)S(1)} %collective-permute-done.4) | copy-start | bytes 24580
  160.0 71.3 %copy-start.19 = (f32[1,1,32,64]{3,2,1,0:T(8,128)}, f32[1,1,32,64]{3,2,1,0:T(8,128)S(1)}, u32[]{:S(2)}) copy-start(f32[1,1,32,64]{3,2,1,0:T(8,128)S(1)} %collective-permute-done.5) | copy-start | bytes 24580
  160.2 71.2 %copy-start.12 = (f32[1,2,32,64]{3,2,1,0:T(8,128)}, f32[1,2,32,64]{3,2,1,0:T(8,128)S(1)}, u32[]{:S(2)}) copy-start(f32[1,2,32,64]{3,2,1,0:T(8,128)S(1)} %get-tuple-element.180) | copy-start | bytes 49156
  160.2 71.2 %copy-start.14 = (f32[1,2,32,64]{3,2,1,0:T(8,128)}, f32[1,2,32,64]{3,2,1,0:T(8,128)S(1)}, u32[]{:S(2)}) copy-start(f32[1,2,32,64]{3,2,1,0:T(8,128)S(1)} %get-tuple-element.181) | copy-start | bytes 49156
  160.2 5.9 %collective-permute-start.8 = (f32[1,1,32,64]{3,2,1,0:T(8,128)S(1)}, f32[1,1,32,64]{3,2,1,0:T(8,128)S(1)}, u32[]{:S(2)}, u32[]{:S(2)}) collective-permute-start(f32[1,1,32,64]{3,2,1,0:T(8,128)S(1)} %get-tuple-element.271), channel_id=1, source_target_pairs={{0,1},{1,2},{2,3},{3,4},{4,5},{5,6},{6,7},{7,8},{8,9},{9,10},{10,1... | collective-permute-start | bytes 24584 | tf_op jit(solution)/shard_map/ppermute | solution.py:23
  162.1 9.0 %collective-permute-start.9 = (f32[1,1,32,64]{3,2,1,0:T(8,128)S(1)}, f32[1,1,32,64]{3,2,1,0:T(8,128)S(1)}, u32[]{:S(2)}, u32[]{:S(2)}) collective-permute-start(f32[1,1,32,64]{3,2,1,0:T(8,128)S(1)} %get-tuple-element.272), channel_id=1, source_target_pairs={{1,0},{2,1},{3,2},{4,3},{5,4},{6,5},{7,6},{8,7},{9,8},{10,9},{11,1... | collective-permute-start | bytes 24584 | tf_op jit(solution)/shard_map/ppermute | solution.py:24
  171.2 5.9 %collective-permute-start.10 = (f32[1,1,32,64]{3,2,1,0:T(8,128)S(1)}, f32[1,1,32,64]{3,2,1,0:T(8,128)S(1)}, u32[]{:S(2)}, u32[]{:S(2)}) collective-permute-start(f32[1,1,32,64]{3,2,1,0:T(8,128)S(1)} %get-tuple-element.265), channel_id=1, source_target_pairs={{0,1},{1,2},{2,3},{3,4},{4,5},{5,6},{6,7},{7,8},{8,9},{9,10},{10,1... | collective-permute-start | bytes 24584 | tf_op jit(solution)/shard_map/ppermute | solution.py:23
  173.1 9.0 %collective-permute-start.11 = (f32[1,1,32,64]{3,2,1,0:T(8,128)S(1)}, f32[1,1,32,64]{3,2,1,0:T(8,128)S(1)}, u32[]{:S(2)}, u32[]{:S(2)}) collective-permute-start(f32[1,1,32,64]{3,2,1,0:T(8,128)S(1)} %get-tuple-element.266), channel_id=1, source_target_pairs={{1,0},{2,1},{3,2},{4,3},{5,4},{6,5},{7,6},{8,7},{9,8},{10,9},{11,1... | collective-permute-start | bytes 24584 | tf_op jit(solution)/shard_map/ppermute | solution.py:24
  231.2 6.9 %copy-start.16 = (f32[1,32,1,32]{3,2,1,0:T(1,128)}, f32[1,32,1,32]{3,2,1,0:T(1,128)S(1)}, u32[]{:S(2)}) copy-start(f32[1,32,1,32]{3,2,1,0:T(1,128)S(1)} %get-tuple-element.224) | copy-start | bytes 12292
  232.0 0.7 copy-start
  232.0 1.6 copy-start.3
  248.6 95.6 %copy-start.1 = (f32[1,32,16,32]{3,2,1,0:T(8,128)S(1)}, f32[1,32,16,32]{3,2,1,0:T(8,128)}, u32[]{:S(2)}) copy-start(f32[1,32,16,32]{3,2,1,0:T(8,128)} %copy-done) | copy-start | bytes 196612
  253.7 0.9 copy-start.2
  342.9 2.8 copy-start.17
  343.9 16.7 %copy-start.9 = (f32[2,32,64]{2,1,0:T(8,128)S(1)}, f32[2,32,64]{2,1,0:T(8,128)}, u32[]{:S(2)}) copy-start(f32[2,32,64]{2,1,0:T(8,128)} %copy-done.8) | copy-start | bytes 49156
  343.9 16.7 %copy-start.11 = (f32[1,2,31,64]{3,2,1,0:T(8,128)S(1)}, f32[1,2,31,64]{3,2,1,0:T(8,128)}, u32[]{:S(2)}) copy-start(f32[1,2,31,64]{3,2,1,0:T(8,128)} %copy-done.10) | copy-start | bytes 47620
  343.9 16.7 %copy-start.13 = (f32[1,2,32,64]{3,2,1,0:T(8,128)S(1)}, f32[1,2,32,64]{3,2,1,0:T(8,128)}, u32[]{:S(2)}) copy-start(f32[1,2,32,64]{3,2,1,0:T(8,128)} %copy-done.12) | copy-start | bytes 49156
  343.9 16.7 %copy-start.15 = (f32[1,2,32,64]{3,2,1,0:T(8,128)S(1)}, f32[1,2,32,64]{3,2,1,0:T(8,128)}, u32[]{:S(2)}) copy-start(f32[1,2,32,64]{3,2,1,0:T(8,128)} %copy-done.14) | copy-start | bytes 49156
  344.0 41.2 %copy-start.5 = (f32[1,1,64,128]{2,3,1,0:T(8,128)S(1)}, f32[1,1,64,128]{2,3,1,0:T(8,128)}, u32[]{:S(2)}) copy-start(f32[1,1,64,128]{2,3,1,0:T(8,128)} %copy-done.4) | copy-start | bytes 98308
  344.0 41.2 %copy-start.7 = (f32[1,1,64,128]{2,3,1,0:T(8,128)S(1)}, f32[1,1,64,128]{2,3,1,0:T(8,128)}, u32[]{:S(2)}) copy-start(f32[1,1,64,128]{2,3,1,0:T(8,128)} %copy-done.6) | copy-start | bytes 98308
  346.9 6.6 %collective-permute-start.12 = (f32[1,1,32,64]{3,2,1,0:T(8,128)S(1)}, f32[1,1,32,64]{3,2,1,0:T(8,128)S(1)}, u32[]{:S(2)}, u32[]{:S(2)}) collective-permute-start(f32[1,1,32,64]{3,2,1,0:T(8,128)S(1)} %get-tuple-element.257), channel_id=1, source_target_pairs={{0,1},{1,2},{2,3},{3,4},{4,5},{5,6},{6,7},{7,8},{8,9},{9,10},{10,1... | collective-permute-start | bytes 24584 | tf_op jit(solution)/shard_map/ppermute | solution.py:23
  351.5 9.1 %collective-permute-start.13 = (f32[1,1,32,64]{3,2,1,0:T(8,128)S(1)}, f32[1,1,32,64]{3,2,1,0:T(8,128)S(1)}, u32[]{:S(2)}, u32[]{:S(2)}) collective-permute-start(f32[1,1,32,64]{3,2,1,0:T(8,128)S(1)} %get-tuple-element.258), channel_id=1, source_target_pairs={{1,0},{2,1},{3,2},{4,3},{5,4},{6,5},{7,6},{8,7},{9,8},{10,9},{11,1... | collective-permute-start | bytes 24584 | tf_op jit(solution)/shard_map/ppermute | solution.py:24
  361.5 5.9 %collective-permute-start.14 = (f32[1,1,32,64]{3,2,1,0:T(8,128)S(1)}, f32[1,1,32,64]{3,2,1,0:T(8,128)S(1)}, u32[]{:S(2)}, u32[]{:S(2)}) collective-permute-start(f32[1,1,32,64]{3,2,1,0:T(8,128)S(1)} %get-tuple-element.251), channel_id=1, source_target_pairs={{0,1},{1,2},{2,3},{3,4},{4,5},{5,6},{6,7},{7,8},{8,9},{9,10},{10,1... | collective-permute-start | bytes 24584 | tf_op jit(solution)/shard_map/ppermute | solution.py:23
  363.5 9.0 %collective-permute-start.15 = (f32[1,1,32,64]{3,2,1,0:T(8,128)S(1)}, f32[1,1,32,64]{3,2,1,0:T(8,128)S(1)}, u32[]{:S(2)}, u32[]{:S(2)}) collective-permute-start(f32[1,1,32,64]{3,2,1,0:T(8,128)S(1)} %get-tuple-element.252), channel_id=1, source_target_pairs={{1,0},{2,1},{3,2},{4,3},{5,4},{6,5},{7,6},{8,7},{9,8},{10,9},{11,1... | collective-permute-start | bytes 24584 | tf_op jit(solution)/shard_map/ppermute | solution.py:24
  373.8 6.2 %collective-permute-start.16 = (f32[1,1,64,128]{2,3,1,0:T(8,128)S(1)}, f32[1,1,64,128]{2,3,1,0:T(8,128)S(1)}, u32[]{:S(2)}, u32[]{:S(2)}) collective-permute-start(f32[1,1,64,128]{2,3,1,0:T(8,128)S(1)} %get-tuple-element.199), channel_id=1, source_target_pairs={{0,1},{1,2},{2,3},{3,4},{4,5},{5,6},{6,7},{7,8},{8,9},{9,10},{10,1... | collective-permute-start | bytes 98312 | tf_op jit(solution)/shard_map/ppermute | solution.py:23
  375.7 9.5 %collective-permute-start.17 = (f32[1,1,64,128]{2,3,1,0:T(8,128)S(1)}, f32[1,1,64,128]{2,3,1,0:T(8,128)S(1)}, u32[]{:S(2)}, u32[]{:S(2)}) collective-permute-start(f32[1,1,64,128]{2,3,1,0:T(8,128)S(1)} %get-tuple-element.200), channel_id=1, source_target_pairs={{1,0},{2,1},{3,2},{4,3},{5,4},{6,5},{7,6},{8,7},{9,8},{10,9},{11,1... | collective-permute-start | bytes 98312 | tf_op jit(solution)/shard_map/ppermute | solution.py:24
  386.5 6.2 %collective-permute-start.18 = (f32[1,1,64,128]{2,3,1,0:T(8,128)S(1)}, f32[1,1,64,128]{2,3,1,0:T(8,128)S(1)}, u32[]{:S(2)}, u32[]{:S(2)}) collective-permute-start(f32[1,1,64,128]{2,3,1,0:T(8,128)S(1)} %get-tuple-element.193), channel_id=1, source_target_pairs={{0,1},{1,2},{2,3},{3,4},{4,5},{5,6},{6,7},{7,8},{8,9},{9,10},{10,1... | collective-permute-start | bytes 98312 | tf_op jit(solution)/shard_map/ppermute | solution.py:23
  388.4 9.5 %collective-permute-start.19 = (f32[1,1,64,128]{2,3,1,0:T(8,128)S(1)}, f32[1,1,64,128]{2,3,1,0:T(8,128)S(1)}, u32[]{:S(2)}, u32[]{:S(2)}) collective-permute-start(f32[1,1,64,128]{2,3,1,0:T(8,128)S(1)} %get-tuple-element.194), channel_id=1, source_target_pairs={{1,0},{2,1},{3,2},{4,3},{5,4},{6,5},{7,6},{8,7},{9,8},{10,9},{11,1... | collective-permute-start | bytes 98312 | tf_op jit(solution)/shard_map/ppermute | solution.py:24
Sparse Core Ops, SparseCore 0:
  9.7 66.4 all-reduce.60
